TPU v7x, 32 devices: a whole 2x2x4 slice. The times are simulated.
32 devices in a mesh: rows: 8 (over y, x, core), snaps: 4 (over z).
Axes of the slice: x: 2, y: 2, z: 4, core: 2. Of those that a mesh axis runs over, the one named last changes fastest.
Arguments:
- snapshots: float32 [2048, 3072], P('rows', 'snaps'), may hold values from -6 to 6
Outputs:
- updated: float32 [2048, 3072], P('rows', 'snaps')
- factor_rows: float32 [1152, 3072], P(None, 'snaps')
All inputs are finite; a program needn't handle non-finite values.
Results may differ from a plain program's by a relative error of at most 0.00013.
Values sent between devices are 32-bit elements; how exact they have to be, the bound alone decides.
A program may use at most 64 MiB of HBM per device.

v0:
```python
import jax
import jax.numpy as jnp
from jax import lax
from jax.sharding import PartitionSpec as P

PANEL = 384
PANELS = 3


def spread(shard, axis, root):
    mine = lax.axis_index(axis) == root
    return lax.psum(jnp.where(mine, shard, jnp.zeros_like(shard)), axis)


def mult(left, right):
    return jnp.dot(left, right, precision=lax.Precision.HIGHEST, preferred_element_type=jnp.float32)


def fetch_panel(section, column_piece, n_snaps):
    return spread(column_piece, "snaps", section % n_snaps)


def shards(snapshots):
    rows_dev, cols_dev = snapshots.shape
    panel_width = PANEL
    n_snaps = lax.axis_size("snaps")
    my_snap = lax.axis_index("snaps")
    local_blocks = cols_dev // panel_width
    row_count = rows_dev * lax.axis_size("rows")
    root_rows = jnp.sqrt(jnp.float32(row_count))
    col_ids = jnp.arange(cols_dev, dtype=jnp.int32)
    turn_cols = col_ids // panel_width * n_snaps + my_snap
    identity = jnp.eye(panel_width, dtype=jnp.float32)
    working = snapshots
    coeff_rows = []
    slot_first = 0
    pending = fetch_panel(0, working[:, slot_first : slot_first + panel_width], n_snaps)
    for section in range(PANELS):
        panel_now = pending
        slot_index = section // n_snaps
        gram_matrix, cross_sums = lax.psum(
            (mult(panel_now.T, panel_now), mult(panel_now.T, working)), "rows"
        )
        factor = jnp.linalg.cholesky(gram_matrix)
        inverse = lax.linalg.triangular_solve(factor, identity, left_side=True, lower=True)
        orthobasis = mult(panel_now, inverse.T)
        coeffs = mult(inverse, cross_sums)
        applied = jnp.where((turn_cols > section)[None, :], coeffs, jnp.float32(0.0))
        working = working - mult(orthobasis, applied)
        low_own = slot_index * panel_width
        is_owner = my_snap == section % n_snaps
        own_cols = jnp.where(
            is_owner, orthobasis * root_rows, working[:, low_own : low_own + panel_width]
        )
        working = working.at[:, low_own : low_own + panel_width].set(own_cols)
        if section + 1 < PANELS:
            next_slot = (section + 1) // n_snaps
            low = next_slot * panel_width
            pending = fetch_panel(section + 1, working[:, low : low + panel_width], n_snaps)
        diagonal = jnp.where(
            (turn_cols == section)[None, :], jnp.tile(factor.T, (1, local_blocks)), jnp.float32(0.0)
        )
        coeff_rows.append((applied + diagonal) / root_rows)
    return (working, jnp.concatenate(coeff_rows, axis=0))


def solution(mesh):
    placed = (P("rows", "snaps"),)
    return jax.shard_map(
        shards,
        mesh=mesh,
        in_specs=placed,
        out_specs=(P("rows", "snaps"), P(None, "snaps")),
        check_vma=False,
    )
```

profile of v0, /device:TPU:0, one launch (start us, length us, event | category | flops | bytes accessed | tf_op | source)
XLA Modules:
  0.0 696.9 jit_solution(14924972085822224887)
XLA Ops:
  9.1 41.5 %all-reduce.11.cloned.1.call-done = f32[256,384]{1,0:T(8,128)} async-done(((f32[256,384]{1,0:T(8,128)}), f32[256,384]{1,0:T(8,128)}) %all-reduce.11.cloned.1.call-update) | async-done | bytes 393232 | tf_op jit(solution)/shard_map/psum | solution.py:12
  50.6 2.8 fusion.82
  56.5 58.8 %all-reduce.21.cloned.1.call-done = (f32[384,384]{0,1:T(8,128)}, f32[384,768]{1,0:T(8,128)}) async-done(((f32[384,384]{0,1:T(8,128)}, f32[384,768]{1,0:T(8,128)}), (f32[384,384]{0,1:T(8,128)}, f32[384,768]{1,0:T(8,128)})) %all-reduce.21.cloned.1.call-update) | async-done | bytes 1769488 | tf_op jit(solution)/shard_map/psum | solution.py:41
  116.8 11.7 %cholesky.273 = f32[128,128]{1,0:T(8,128)S(1)} custom-call(f32[128,128]{1,0:T(8,128)S(1)} %cholesky.428), custom_call_target="Cholesky" | custom-call | tf_op jit(solution)/shard_map/jit(cholesky)/cholesky | solution.py:44
  128.6 9.8 %custom-call.23 = f32[1,128,128]{1,2,0:T(8,128)S(1)} custom-call(f32[1,128,128]{2,1,0:T(8,128)S(1)} %get-tuple-element.129), custom_call_target="InvertDiagBlocksLowerTriangular" | custom-call | tf_op jit(solution)/shard_map/jit(cholesky)/cholesky | solution.py:44
  139.0 11.7 %cholesky.292 = f32[128,128]{1,0:T(8,128)S(1)} custom-call(f32[128,128]{1,0:T(8,128)S(1)} %cholesky.432), custom_call_target="Cholesky" | custom-call | tf_op jit(solution)/shard_map/jit(cholesky)/cholesky | solution.py:44
  150.7 10.0 %custom-call.24 = f32[1,128,128]{1,2,0:T(8,128)S(1)} custom-call(f32[1,128,128]{2,1,0:T(8,128)S(1)} %get-tuple-element.126), custom_call_target="InvertDiagBlocksLowerTriangular" | custom-call | tf_op jit(solution)/shard_map/jit(cholesky)/cholesky | solution.py:44
  161.2 11.7 %cholesky.311 = f32[128,128]{1,0:T(8,128)S(1)} custom-call(f32[128,128]{1,0:T(8,128)S(1)} %convolution_subtract_fusion.14), custom_call_target="Cholesky" | custom-call | tf_op jit(solution)/shard_map/jit(cholesky)/cholesky | solution.py:44
  176.4 6.0 while.9
  183.2 29.9 %custom-call.25 = f32[3,128,128]{1,2,0:T(8,128)S(1)} custom-call(f32[3,128,128]{2,1,0:T(8,128)S(1)} %get-tuple-element.60), custom_call_target="InvertDiagBlocksLowerTriangular" | custom-call | tf_op jit(solution)/shard_map/triangular_solve/custom-call.2 | solution.py:45
  224.6 36.4 %all-reduce.13.cloned.1.call-done = f32[256,384]{1,0:T(8,128)} async-done(((f32[256,384]{1,0:T(8,128)}), f32[256,384]{1,0:T(8,128)}) %all-reduce.13.cloned.1.call-update) | async-done | bytes 393232 | tf_op jit(solution)/shard_map/psum | solution.py:12
  261.0 2.8 fusion.84
  266.2 59.5 %all-reduce.19.cloned.1.call-done = (f32[384,384]{0,1:T(8,128)}, f32[384,768]{1,0:T(8,128)}) async-done(((f32[384,384]{0,1:T(8,128)}, f32[384,768]{1,0:T(8,128)}), (f32[384,384]{0,1:T(8,128)}, f32[384,768]{1,0:T(8,128)})) %all-reduce.19.cloned.1.call-update) | async-done | bytes 1769488 | tf_op jit(solution)/shard_map/psum | solution.py:41
  330.0 11.7 %cholesky.326 = f32[128,128]{1,0:T(8,128)S(1)} custom-call(f32[128,128]{1,0:T(8,128)S(1)} %cholesky.436), custom_call_target="Cholesky" | custom-call | tf_op jit(solution)/shard_map/jit(cholesky)/cholesky | solution.py:44
  342.6 9.8 %custom-call.26 = f32[1,128,128]{1,2,0:T(8,128)S(1)} custom-call(f32[1,128,128]{2,1,0:T(8,128)S(1)} %get-tuple-element.122), custom_call_target="InvertDiagBlocksLowerTriangular" | custom-call | tf_op jit(solution)/shard_map/jit(cholesky)/cholesky | solution.py:44
  355.4 11.7 %cholesky.345 = f32[128,128]{1,0:T(8,128)S(1)} custom-call(f32[128,128]{1,0:T(8,128)S(1)} %cholesky.440), custom_call_target="Cholesky" | custom-call | tf_op jit(solution)/shard_map/jit(cholesky)/cholesky | solution.py:44
  367.7 10.2 %custom-call.27 = f32[1,128,128]{1,2,0:T(8,128)S(1)} custom-call(f32[1,128,128]{2,1,0:T(8,128)S(1)} %get-tuple-element.119), custom_call_target="InvertDiagBlocksLowerTriangular" | custom-call | tf_op jit(solution)/shard_map/jit(cholesky)/cholesky | solution.py:44
  380.0 11.7 %cholesky.364 = f32[128,128]{1,0:T(8,128)S(1)} custom-call(f32[128,128]{1,0:T(8,128)S(1)} %convolution_subtract_fusion.13), custom_call_target="Cholesky" | custom-call | tf_op jit(solution)/shard_map/jit(cholesky)/cholesky | solution.py:44
  398.4 8.7 %while.10 = (s32[]{:T(128)}, f32[384,384]{1,0:T(8,128)}, s32[3,2]{0,1:T(2,128)S(1)}, f32[3,128,128]{2,1,0:T(8,128)S(1)}, s32[]{:T(128)}) while((s32[]{:T(128)}, f32[384,384]{1,0:T(8,128)}, s32[3,2]{0,1:T(2,128)S(1)}, f32[3,128,128]{2,1,0:T(8,128)S(1)}, s32[]{:T(128)}) %tuple.117), condition=%wide.while_cond.3.clone, body=%wide.while_body.3.clone.sunk | while | flops 2 | bytes 131189 | solution.py:45
  407.1 29.5 %custom-call.28 = f32[3,128,128]{1,2,0:T(8,128)S(1)} custom-call(f32[3,128,128]{2,1,0:T(8,128)S(1)} %get-tuple-element.61), custom_call_target="InvertDiagBlocksLowerTriangular" | custom-call | tf_op jit(solution)/shard_map/triangular_solve/custom-call.2 | solution.py:45
  445.9 3.1 add_multiply_fusion.1
  453.1 36.2 %all-reduce.15.cloned.1.call-done = f32[256,384]{1,0:T(8,128)} async-done(((f32[256,384]{1,0:T(8,128)}), f32[256,384]{1,0:T(8,128)}) %all-reduce.15.cloned.1.call-update) | async-done | bytes 393232 | tf_op jit(solution)/shard_map/psum | solution.py:12
  489.3 2.8 fusion.86
  494.4 59.7 %all-reduce.17.cloned.1.call-done = (f32[384,384]{0,1:T(8,128)}, f32[384,768]{1,0:T(8,128)}) async-done(((f32[384,384]{0,1:T(8,128)}, f32[384,768]{1,0:T(8,128)}), (f32[384,384]{0,1:T(8,128)}, f32[384,768]{1,0:T(8,128)})) %all-reduce.17.cloned.1.call-update) | async-done | bytes 1769488 | tf_op jit(solution)/shard_map/psum | solution.py:41
  558.2 11.7 %cholesky.379 = f32[128,128]{1,0:T(8,128)S(1)} custom-call(f32[128,128]{1,0:T(8,128)S(1)} %cholesky.444), custom_call_target="Cholesky" | custom-call | tf_op jit(solution)/shard_map/jit(cholesky)/cholesky | solution.py:44
  572.1 11.3 %custom-call.29 = f32[1,128,128]{1,2,0:T(8,128)} custom-call(f32[1,128,128]{2,1,0:T(8,128)} %get-tuple-element.115), custom_call_target="InvertDiagBlocksLowerTriangular" | custom-call | tf_op jit(solution)/shard_map/jit(cholesky)/cholesky | solution.py:44
  587.0 13.3 %cholesky.398 = f32[128,128]{1,0:T(8,128)} custom-call(f32[128,128]{1,0:T(8,128)} %cholesky.448), custom_call_target="Cholesky" | custom-call | tf_op jit(solution)/shard_map/jit(cholesky)/cholesky | solution.py:44
  602.3 11.3 %custom-call.30 = f32[1,128,128]{1,2,0:T(8,128)} custom-call(f32[1,128,128]{2,1,0:T(8,128)} %get-tuple-element.112), custom_call_target="InvertDiagBlocksLowerTriangular" | custom-call | tf_op jit(solution)/shard_map/jit(cholesky)/cholesky | solution.py:44
  616.4 13.2 %cholesky.417 = f32[128,128]{1,0:T(8,128)} custom-call(f32[128,128]{1,0:T(8,128)} %convolution_subtract_fusion.12), custom_call_target="Cholesky" | custom-call | tf_op jit(solution)/shard_map/jit(cholesky)/cholesky | solution.py:44
  636.1 8.8 %while.11 = (s32[]{:T(128)}, f32[384,384]{1,0:T(8,128)}, s32[3,2]{0,1:T(2,128)S(1)}, f32[3,128,128]{2,1,0:T(8,128)S(1)}, s32[]{:T(128)}) while((s32[]{:T(128)}, f32[384,384]{1,0:T(8,128)}, s32[3,2]{0,1:T(2,128)S(1)}, f32[3,128,128]{2,1,0:T(8,128)S(1)}, s32[]{:T(128)}) %tuple.118), condition=%wide.while_cond.3.clone.1, body=%wide.while_body.3.clone.1.sunk | while | flops 2 | bytes 131189 | solution.py:45
  637.0 2.2 bitcast_dynamic-update-slice_fusion.8
  645.0 29.5 %custom-call.31 = f32[3,128,128]{1,2,0:T(8,128)S(1)} custom-call(f32[3,128,128]{2,1,0:T(8,128)S(1)} %get-tuple-element.62), custom_call_target="InvertDiagBlocksLowerTriangular" | custom-call | tf_op jit(solution)/shard_map/triangular_solve/custom-call.2 | solution.py:45
  (171 shorter events, 110.2 us)
Async XLA Ops:
  7.2 43.5 %all-reduce.11.cloned.1.call-start = ((), (), s32[]{:S(2)}) async-start(), calls=%async_computation | async-start | bytes 786432 | tf_op jit(solution)/shard_map/psum | solution.py:12
  7.2 46.2 %copy-start.3 = (f32[256,768]{1,0:T(8,128)S(1)}, f32[256,768]{1,0:T(8,128)}, u32[]{:S(2)}) copy-start(f32[256,768]{1,0:T(8,128)} %param.10) | copy-start | bytes 2359300
  9.1 106.2 %all-reduce.21.cloned.1.call-start = ((), (), s32[]{:S(2)}) async-start(), calls=%async_computation.5 | async-start | bytes 3538944 | tf_op jit(solution)/shard_map/psum | solution.py:41
  50.6 2.8 copy-start
  55.6 205.4 %all-reduce.13.cloned.1.call-start = ((), (), s32[]{:S(2)}) async-start(), calls=%async_computation.1 | async-start | bytes 786432 | tf_op jit(solution)/shard_map/psum | solution.py:12
  115.3 1.4 copy-start.5
  182.4 0.8 copy-start.7
  217.3 1.3 copy-start.11
  224.6 101.1 %all-reduce.19.cloned.1.call-start = ((), (), s32[]{:S(2)}) async-start(), calls=%async_computation.4 | async-start | bytes 3538944 | tf_op jit(solution)/shard_map/psum | solution.py:41
  261.0 2.8 copy-start.1
  266.0 223.4 %all-reduce.15.cloned.1.call-start = ((), (), s32[]{:S(2)}) async-start(), calls=%async_computation.2 | async-start | bytes 786432 | tf_op jit(solution)/shard_map/psum | solution.py:12
  329.1 0.8 copy-start.9
  436.6 1.9 copy-start.17
  444.7 1.3 copy-start.12
  452.9 101.2 %all-reduce.17.cloned.1.call-start = ((), (), s32[]{:S(2)}) async-start(), calls=%async_computation.3 | async-start | bytes 3538944 | tf_op jit(solution)/shard_map/psum | solution.py:41
  489.3 2.8 copy-start.2
  554.1 2.2 copy-start.6
  557.4 0.8 copy-start.10
  570.0 0.6 copy-start.15
  585.7 0.7 copy-start.14
  674.5 1.9 copy-start.16
  680.6 1.3 copy-start.13
  686.4 1.3 copy-start.4
  687.2 2.5 copy-start.8
Sparse Core Ops, SparseCore 0:
  10.9 39.6 all-reduce.10
  55.7 59.5 all-reduce.20
  224.7 36.2 all-reduce.12
  266.1 59.5 all-reduce.18
  453.0 36.2 all-reduce.14
  494.5 59.5 all-reduce.16
where the time goes:
time: 701 us; the launch traced here: 697 us
  waiting for transfers between devices  292 us (42%)
  other arithmetic  285 us (41%)
  matrix products  53.1 us (8%)
  local copies, waits for them, and re-layouts  45.1 us (6%)
  between operations  20.7 us (3%)
    another operation x32, other arithmetic, shards(): factor = jnp.linalg.cholesky(gram_matrix)  182 us
    psum x3, waiting for transfers between devices, shards(): lax.psum((mult(panel_now.T, panel_now), mult(panel_now.T, working)), 'rows')  178 us
    psum x3, waiting for transfers between devices, spread(): return lax.psum(jnp.where(mine, shard, jnp.zeros_like(shard)), axis)  114 us
    another operation x4, other arithmetic, shards(): lax.linalg.triangular_solve(factor, identity, left_side=True, lower=True)  88.9 us
    dot_general x15, matrix products, mult(): jnp.dot(left, right, precision=lax.Precision.HIGHEST, preferred_element_t...  29.4 us
    another operation x31, local copies, waits for them, and re-layouts, shards(): lax.linalg.triangular_solve(factor, identity, left_side=True, lower=True)  23.1 us
  transfers between devices with their start and end apart: 6, of which 6 were waited for; matrix products, arithmetic and copies ran while one was open for 0% of the time, Pallas kernels for 0%

commit v1 on v0

--- a/solution.py
+++ b/solution.py
@@ -9,7 +9,7 @@
 
 def spread(shard, axis, root):
     mine = lax.axis_index(axis) == root
-    return lax.psum(jnp.where(mine, shard, jnp.zeros_like(shard)), axis)
+    return jnp.sum(lax.all_gather(jnp.where(mine, shard, jnp.zeros_like(shard)), axis), axis=0)
 
 
 def mult(left, right):

time: 701 us -> 671 us (0.957)
  other arithmetic: 285 us -> 275 us
  local copies, waits for them, and re-layouts: 45.1 us -> 36.2 us
  matrix products: 53.1 us -> 45 us
    psum x3 -> x0, waiting for transfers between devices: 114 us -> none  [spread(): return lax.psum(jnp.where(mine, shard, jnp.zeros_like(shard)), axis)]
    all_gather x0 -> x3, waiting for transfers between devices: none -> 114 us  [spread(): lax.all_gather(jnp.where(mine, shard, jnp.zeros_like(shard)), axis)]
    another operation x32, other arithmetic: 182 us -> 171 us  [shards(): factor = jnp.linalg.cholesky(gram_matrix)]
where the time goes in v1:
time: 671 us; the launch traced here: 667 us
  waiting for transfers between devices  289 us (43%)
  other arithmetic  275 us (41%)
  matrix products  45 us (7%)
  local copies, waits for them, and re-layouts  36.2 us (5%)
  between operations  20.7 us (3%)
    psum x3, waiting for transfers between devices, shards(): lax.psum((mult(panel_now.T, panel_now), mult(panel_now.T, working)), 'rows')  176 us
    another operation x32, other arithmetic, shards(): factor = jnp.linalg.cholesky(gram_matrix)  171 us
    all_gather x3, waiting for transfers between devices, spread(): lax.all_gather(jnp.where(mine, shard, jnp.zeros_like(shard)), axis)  114 us
    another operation x4, other arithmetic, shards(): lax.linalg.triangular_solve(factor, identity, left_side=True, lower=True)  88.9 us
    dot_general x15, matrix products, mult(): jnp.dot(left, right, precision=lax.Precision.HIGHEST, preferred_element_t...  27.7 us
    another operation x31, local copies, waits for them, and re-layouts, shards(): lax.linalg.triangular_solve(factor, identity, left_side=True, lower=True)  23.1 us
  transfers between devices with their start and end apart: 6, of which 6 were waited for; matrix products, arithmetic and copies ran while one was open for 0% of the time, Pallas kernels for 0%

profile of v1, /device:TPU:0, one launch (start us, length us, event | category | flops | bytes accessed | tf_op | source)
XLA Modules:
  0.0 667.4 jit_solution(10819419880143934225)
XLA Ops:
  9.1 40.8 %all-gather.7.cloned.1.call-done = f32[1024,384]{1,0:T(8,128)} async-done(((f32[256,384]{1,0:T(8,128)}), f32[1024,384]{1,0:T(8,128)}) %all-gather.7.cloned.1.call-update) | async-done | bytes 1572880 | tf_op jit(solution)/shard_map/all_gather | solution.py:12
  56.2 58.0 %all-reduce.12.cloned.1.call-done = (f32[384,384]{0,1:T(8,128)}, f32[384,768]{1,0:T(8,128)}) async-done(((f32[384,384]{0,1:T(8,128)}, f32[384,768]{1,0:T(8,128)}), (f32[384,384]{0,1:T(8,128)}, f32[384,768]{1,0:T(8,128)})) %all-reduce.12.cloned.1.call-update) | async-done | bytes 1769488 | tf_op jit(solution)/shard_map/psum | solution.py:41
  116.5 11.7 %cholesky.273 = f32[128,128]{1,0:T(8,128)S(1)} custom-call(f32[128,128]{1,0:T(8,128)S(1)} %cholesky.428), custom_call_target="Cholesky" | custom-call | tf_op jit(solution)/shard_map/jit(cholesky)/cholesky | solution.py:44
  128.3 9.8 %custom-call.23 = f32[1,128,128]{1,2,0:T(8,128)S(1)} custom-call(f32[1,128,128]{2,1,0:T(8,128)S(1)} %get-tuple-element.129), custom_call_target="InvertDiagBlocksLowerTriangular" | custom-call | tf_op jit(solution)/shard_map/jit(cholesky)/cholesky | solution.py:44
  140.5 11.7 %cholesky.292 = f32[128,128]{1,0:T(8,128)S(1)} custom-call(f32[128,128]{1,0:T(8,128)S(1)} %cholesky.432), custom_call_target="Cholesky" | custom-call | tf_op jit(solution)/shard_map/jit(cholesky)/cholesky | solution.py:44
  152.2 10.0 %custom-call.24 = f32[1,128,128]{1,2,0:T(8,128)S(1)} custom-call(f32[1,128,128]{2,1,0:T(8,128)S(1)} %get-tuple-element.126), custom_call_target="InvertDiagBlocksLowerTriangular" | custom-call | tf_op jit(solution)/shard_map/jit(cholesky)/cholesky | solution.py:44
  163.5 11.7 %cholesky.311 = f32[128,128]{1,0:T(8,128)S(1)} custom-call(f32[128,128]{1,0:T(8,128)S(1)} %convolution_subtract_fusion.14), custom_call_target="Cholesky" | custom-call | tf_op jit(solution)/shard_map/jit(cholesky)/cholesky | solution.py:44
  179.4 8.7 %while.9 = (s32[]{:T(128)}, f32[384,384]{1,0:T(8,128)}, s32[3,2]{0,1:T(2,128)S(1)}, f32[3,128,128]{2,1,0:T(8,128)S(1)}, s32[]{:T(128)}) while((s32[]{:T(128)}, f32[384,384]{1,0:T(8,128)}, s32[3,2]{0,1:T(2,128)S(1)}, f32[3,128,128]{2,1,0:T(8,128)S(1)}, s32[]{:T(128)}) %tuple.93), condition=%wide.while_cond.3, body=%wide.while_body.3.sunk | while | flops 2 | bytes 131189 | solution.py:45
  180.1 2.3 bitcast_dynamic-update-slice_fusion.6
  183.0 2.3 bitcast_dynamic-update-slice_fusion.6
  188.1 29.9 %custom-call.25 = f32[3,128,128]{1,2,0:T(8,128)S(1)} custom-call(f32[3,128,128]{2,1,0:T(8,128)S(1)} %get-tuple-element.60), custom_call_target="InvertDiagBlocksLowerTriangular" | custom-call | tf_op jit(solution)/shard_map/triangular_solve/custom-call.2 | solution.py:45
  225.2 3.1 add_multiply_fusion.2
  231.3 36.4 %all-gather.9.cloned.1.call-done = f32[1024,384]{1,0:T(8,128)} async-done(((f32[256,384]{1,0:T(8,128)}), f32[1024,384]{1,0:T(8,128)}) %all-gather.9.cloned.1.call-update) | async-done | bytes 1572880 | tf_op jit(solution)/shard_map/all_gather | solution.py:12
  273.4 58.7 %all-reduce.10.cloned.1.call-done = (f32[384,384]{0,1:T(8,128)}, f32[384,768]{1,0:T(8,128)}) async-done(((f32[384,384]{0,1:T(8,128)}, f32[384,768]{1,0:T(8,128)}), (f32[384,384]{0,1:T(8,128)}, f32[384,768]{1,0:T(8,128)})) %all-reduce.10.cloned.1.call-update) | async-done | bytes 1769488 | tf_op jit(solution)/shard_map/psum | solution.py:41
  333.6 11.7 %cholesky.326 = f32[128,128]{1,0:T(8,128)S(1)} custom-call(f32[128,128]{1,0:T(8,128)S(1)} %cholesky.436), custom_call_target="Cholesky" | custom-call | tf_op jit(solution)/shard_map/jit(cholesky)/cholesky | solution.py:44
  345.4 9.8 %custom-call.26 = f32[1,128,128]{1,2,0:T(8,128)S(1)} custom-call(f32[1,128,128]{2,1,0:T(8,128)S(1)} %get-tuple-element.122), custom_call_target="InvertDiagBlocksLowerTriangular" | custom-call | tf_op jit(solution)/shard_map/jit(cholesky)/cholesky | solution.py:44
  355.7 11.7 %cholesky.345 = f32[128,128]{1,0:T(8,128)S(1)} custom-call(f32[128,128]{1,0:T(8,128)S(1)} %cholesky.440), custom_call_target="Cholesky" | custom-call | tf_op jit(solution)/shard_map/jit(cholesky)/cholesky | solution.py:44
  367.5 10.2 %custom-call.27 = f32[1,128,128]{1,2,0:T(8,128)S(1)} custom-call(f32[1,128,128]{2,1,0:T(8,128)S(1)} %get-tuple-element.119), custom_call_target="InvertDiagBlocksLowerTriangular" | custom-call | tf_op jit(solution)/shard_map/jit(cholesky)/cholesky | solution.py:44
  378.2 11.7 %cholesky.364 = f32[128,128]{1,0:T(8,128)S(1)} custom-call(f32[128,128]{1,0:T(8,128)S(1)} %convolution_subtract_fusion.13), custom_call_target="Cholesky" | custom-call | tf_op jit(solution)/shard_map/jit(cholesky)/cholesky | solution.py:44
  394.6 5.8 while.10
  400.4 29.5 %custom-call.28 = f32[3,128,128]{1,2,0:T(8,128)S(1)} custom-call(f32[3,128,128]{2,1,0:T(8,128)S(1)} %get-tuple-element.61), custom_call_target="InvertDiagBlocksLowerTriangular" | custom-call | tf_op jit(solution)/shard_map/triangular_solve/custom-call.2 | solution.py:45
  435.7 3.1 add_multiply_fusion.1
  441.9 36.2 %all-gather.11.cloned.1.call-done = f32[1024,384]{1,0:T(8,128)} async-done(((f32[256,384]{1,0:T(8,128)}), f32[1024,384]{1,0:T(8,128)}) %all-gather.11.cloned.1.call-update) | async-done | bytes 1572880 | tf_op jit(solution)/shard_map/all_gather | solution.py:12
  483.6 58.9 %all-reduce.8.cloned.1.call-done = (f32[384,384]{0,1:T(8,128)}, f32[384,768]{1,0:T(8,128)}) async-done(((f32[384,384]{0,1:T(8,128)}, f32[384,768]{1,0:T(8,128)}), (f32[384,384]{0,1:T(8,128)}, f32[384,768]{1,0:T(8,128)})) %all-reduce.8.cloned.1.call-update) | async-done | bytes 1769488 | tf_op jit(solution)/shard_map/psum | solution.py:41
  544.7 11.7 %cholesky.379 = f32[128,128]{1,0:T(8,128)S(1)} custom-call(f32[128,128]{1,0:T(8,128)S(1)} %cholesky.444), custom_call_target="Cholesky" | custom-call | tf_op jit(solution)/shard_map/jit(cholesky)/cholesky | solution.py:44
  556.5 9.8 %custom-call.29 = f32[1,128,128]{1,2,0:T(8,128)S(1)} custom-call(f32[1,128,128]{2,1,0:T(8,128)S(1)} %get-tuple-element.115), custom_call_target="InvertDiagBlocksLowerTriangular" | custom-call | tf_op jit(solution)/shard_map/jit(cholesky)/cholesky | solution.py:44
  568.7 11.9 %cholesky.398 = f32[128,128]{1,0:T(8,128)S(1)} custom-call(f32[128,128]{1,0:T(8,128)S(1)} %cholesky.448), custom_call_target="Cholesky" | custom-call | tf_op jit(solution)/shard_map/jit(cholesky)/cholesky | solution.py:44
  580.7 9.8 %custom-call.30 = f32[1,128,128]{1,2,0:T(8,128)S(1)} custom-call(f32[1,128,128]{2,1,0:T(8,128)S(1)} %get-tuple-element.112), custom_call_target="InvertDiagBlocksLowerTriangular" | custom-call | tf_op jit(solution)/shard_map/jit(cholesky)/cholesky | solution.py:44
  591.8 11.7 %cholesky.417 = f32[128,128]{1,0:T(8,128)S(1)} custom-call(f32[128,128]{1,0:T(8,128)S(1)} %convolution_subtract_fusion.12), custom_call_target="Cholesky" | custom-call | tf_op jit(solution)/shard_map/jit(cholesky)/cholesky | solution.py:44
  608.4 9.0 %while.11 = (s32[]{:T(128)}, f32[384,384]{1,0:T(8,128)}, s32[3,2]{0,1:T(2,128)S(1)}, f32[3,128,128]{2,1,0:T(8,128)S(1)}, s32[]{:T(128)}) while((s32[]{:T(128)}, f32[384,384]{1,0:T(8,128)}, s32[3,2]{0,1:T(2,128)S(1)}, f32[3,128,128]{2,1,0:T(8,128)S(1)}, s32[]{:T(128)}) %tuple.118), condition=%wide.while_cond.3.clone.1, body=%wide.while_body.3.clone.1.sunk | while | flops 2 | bytes 131189 | solution.py:45
  612.2 2.2 bitcast_dynamic-update-slice_fusion.8
  617.4 29.5 %custom-call.31 = f32[3,128,128]{1,2,0:T(8,128)S(1)} custom-call(f32[3,128,128]{2,1,0:T(8,128)S(1)} %get-tuple-element.62), custom_call_target="InvertDiagBlocksLowerTriangular" | custom-call | tf_op jit(solution)/shard_map/triangular_solve/custom-call.2 | solution.py:45
  (164 shorter events, 90.1 us)
Async XLA Ops:
  7.2 42.7 %all-gather.7.cloned.1.call-start = ((), (), s32[]{:S(2)}) async-start(), calls=%async_computation | async-start | bytes 1966080 | tf_op jit(solution)/shard_map/all_gather | solution.py:12
  9.0 105.2 %all-reduce.12.cloned.1.call-start = ((), (), s32[]{:S(2)}) async-start(), calls=%async_computation.5 | async-start | bytes 3538944 | tf_op jit(solution)/shard_map/psum | solution.py:41
  51.4 1.7 copy-start
  55.3 212.5 %all-gather.9.cloned.1.call-start = ((), (), s32[]{:S(2)}) async-start(), calls=%async_computation.1 | async-start | bytes 1966080 | tf_op jit(solution)/shard_map/all_gather | solution.py:12
  114.2 1.4 copy-start.4
  115.7 0.8 copy-start.8
  223.9 1.3 copy-start.10
  225.2 3.1 copy-start.3
  231.3 100.8 %all-reduce.10.cloned.1.call-start = ((), (), s32[]{:S(2)}) async-start(), calls=%async_computation.4 | async-start | bytes 3538944 | tf_op jit(solution)/shard_map/psum | solution.py:41
  273.2 205.0 %all-gather.11.cloned.1.call-start = ((), (), s32[]{:S(2)}) async-start(), calls=%async_computation.2 | async-start | bytes 1966080 | tf_op jit(solution)/shard_map/all_gather | solution.py:12
  332.1 1.4 copy-start.5
  434.4 1.3 copy-start.11
  441.7 100.8 %all-reduce.8.cloned.1.call-start = ((), (), s32[]{:S(2)}) async-start(), calls=%async_computation.3 | async-start | bytes 3538944 | tf_op jit(solution)/shard_map/psum | solution.py:41
  542.5 1.4 copy-start.6
  543.9 0.8 copy-start.9
  652.0 1.3 copy-start.12
  655.5 2.3 copy-start.2
  656.9 1.3 copy-start.1
  657.7 2.5 copy-start.7
Sparse Core Ops, SparseCore 0:
  10.1 39.7 all-gather.6
  55.4 58.7 all-reduce.11
  231.4 36.3 all-gather.8
  273.3 58.7 all-reduce.9
  441.8 36.3 all-gather.10
  483.7 58.7 all-reduce.7
